TPU v7x, 512 devices: a whole 4x8x8 slice. The times are simulated.
512 devices in a mesh: sec: 16 (over z_hi, y), term: 32 (over z_lo, x, core).
Axes of the slice: x: 4, y: 8, z: 8 (z_hi: 2, z_lo: 4; z = z_hi * 4 + z_lo), core: 2. Of those that a mesh axis runs over, the one named last changes fastest.
Arguments:
- psi: bfloat16 [32, 2, 512, 512], P('sec'), may hold values from -6 to 6
- left_ops: bfloat16 [32, 32, 512, 512], P('term', 'sec'), may hold values from -0.25 to 0.25
- right_ops: bfloat16 [32, 32, 512, 512], P('term', 'sec'), may hold values from -0.046875 to 0.046875
- shift: int32 [32], P('term'), may hold values from -2 to 2, as said below
- live: int32 [32], P('term'), may hold values 0 or 1
Outputs:
- sigma: bfloat16 [32, 2, 512, 512], P('sec', None, 'term')
Inputs may be any that keep to these rules, and one draw needn't show every extreme that they name: `shift`: every draw holds both -2 and 2.
All inputs are finite; a program needn't handle non-finite values. No bound on the sum of `live` on one device may be relied on, other than what follows from the above.
Results may differ from a plain program's by a relative error of at most 0.0049.
Values may be sent and summed in bfloat16 or wider, within the bound.
A program may use at most 64 MiB of HBM per device.

v0:
```python
import jax
import jax.numpy as jnp
from jax import lax
from jax.sharding import PartitionSpec as P

DQ = 2


def padded_2(block, sides, width):
    for axis, dim in sides:
        count = lax.axis_size(axis)
        forward = [(i, i + 1) for i in range(count - 1)]
        backward = [(target, source) for source, target in forward]
        low = lax.ppermute(
            lax.slice_in_dim(block, block.shape[dim] - width, None, axis=dim), axis, forward
        )
        high = lax.ppermute(lax.slice_in_dim(block, 0, width, axis=dim), axis, backward)
        block = jnp.concatenate([low, block, high], axis=dim)
    return block


def local(psi, left_ops, right_ops, shift, live):
    sec_count = psi.shape[0]
    padded = padded_2(psi, (("sec", 0),), DQ)
    left_rows = left_ops[0]
    block = lax.dynamic_slice_in_dim(padded, DQ - shift[0], sec_count, 0)
    inner = jnp.einsum(
        "sab,svbc->asvc", left_rows, block, preferred_element_type=jnp.float32
    ).astype(jnp.bfloat16)
    acc = jnp.einsum(
        "asvc,sdc->asvd", inner, right_ops[0], preferred_element_type=jnp.float32
    ) * live[0].astype(jnp.float32)
    summed = lax.psum_scatter(acc, "term", scatter_dimension=0, tiled=True)
    return jnp.transpose(summed, (1, 2, 0, 3)).astype(jnp.bfloat16)


def solution(mesh):
    in_specs = (
        P("sec", None, None, None),
        P("term", "sec", None, None),
        P("term", "sec", None, None),
        P("term"),
        P("term"),
    )
    out_specs = P("sec", None, "term", None)
    return jax.shard_map(local, mesh=mesh, in_specs=in_specs, out_specs=out_specs, check_vma=False)
```

profile of v0, /device:TPU:56, one launch (start us, length us, event | category | flops | bytes accessed | tf_op | source)
XLA Modules:
  0.0 280.7 jit_solution(17639417792540183379)
XLA Ops:
  6.5 0.0 copy-start
  6.5 0.0 reduce-scatter.2.cloned.1.call-start
  6.5 10.2 %collective-permute-start = (bf16[2,2,512,512]{3,2,1,0:T(8,128)(2,1)}, bf16[2,2,512,512]{3,2,1,0:T(8,128)(2,1)S(1)}, u32[]{:S(2)}, u32[]{:S(2)}) collective-permute-start(bf16[2,2,512,512]{3,2,1,0:T(8,128)(2,1)} %param.5), channel_id=1, source_target_pairs={{0,32},{32,64},{64,96},{96,128},{128,160},{160,192},{192,224},{224... | collective-permute-start | bytes 6291464 | tf_op jit(solution)/shard_map/ppermute | solution.py:14
  16.8 1.9 collective-permute-start.1
  20.0 79.7 %collective-permute-done = bf16[2,2,512,512]{3,2,1,0:T(8,128)(2,1)S(1)} collective-permute-done((bf16[2,2,512,512]{3,2,1,0:T(8,128)(2,1)}, bf16[2,2,512,512]{3,2,1,0:T(8,128)(2,1)S(1)}, u32[]{:S(2)}, u32[]{:S(2)}) %collective-permute-start) | collective-permute-done | bytes 2097184 | tf_op jit(solution)/shard_map/ppermute | solution.py:14
  99.7 14.0 %collective-permute-done.1 = bf16[2,2,512,512]{3,2,1,0:T(8,128)(2,1)} collective-permute-done((bf16[2,2,512,512]{3,2,1,0:T(8,128)(2,1)}, bf16[2,2,512,512]{3,2,1,0:T(8,128)(2,1)}, u32[]{:S(2)}, u32[]{:S(2)}) %collective-permute-start.1) | collective-permute-done | bytes 2097184 | tf_op jit(solution)/shard_map/ppermute | solution.py:17
  113.7 0.0 copy-done
  113.7 6.5 %multiply_bitcast_fusion = f32[512,2,2,512]{3,0,2,1:T(8,128)} fusion(f32[]{:T(128)} %bitcast.9, s32[]{:T(128)S(6)} %select_n.3, bf16[2,2,512,512]{3,2,1,0:T(8,128)(2,1)S(1)} %collective-permute-done, bf16[2,2,512,512]{3,2,1,0:T(8,128)(2,1)} %param.5, bf16[2,2,512,512]{3,2,1,0:T(8,128)(2,1)} %collective-permute-done.1, ...), kind=kOutput, calls=%fused_computation.3 | convolution fusion | flops 2155872256 | bytes 12582920 | tf_op jit(solution)/shard_map/asvc,sdc->asvd/dot_general | solution.py:30
  120.2 0.0 reduce-scatter.2.cloned.1.call-update
  120.2 152.1 %reduce-scatter.2.cloned.1.call-done = f32[16,2,2,512]{3,0,2,1:T(8,128)} async-done(((f32[512,2,2,512]{3,0,2,1:T(8,128)}), f32[16,2,2,512]{3,0,2,1:T(8,128)}) %reduce-scatter.2.cloned.1.call-update) | async-done | bytes 131088 | tf_op jit(solution)/shard_map/reduce_scatter | solution.py:33
  272.3 1.5 convert_bitcast_fusion
Async XLA Ops:
  6.5 107.2 %copy-start = (bf16[1,2,512,512]{3,2,1,0:T(8,128)(2,1)S(1)}, bf16[1,2,512,512]{3,2,1,0:T(8,128)(2,1)}, u32[]{:S(2)}) copy-start(bf16[1,2,512,512]{3,2,1,0:T(8,128)(2,1)} %param.7) | copy-start | bytes 3145732
  6.5 265.8 %reduce-scatter.2.cloned.1.call-start = ((), (), s32[]{:S(2)}) async-start(), calls=%async_computation.1 | async-start | bytes 4325376 | tf_op jit(solution)/shard_map/reduce_scatter | solution.py:33
  6.5 93.2 %collective-permute-start = (bf16[2,2,512,512]{3,2,1,0:T(8,128)(2,1)}, bf16[2,2,512,512]{3,2,1,0:T(8,128)(2,1)S(1)}, u32[]{:S(2)}, u32[]{:S(2)}) collective-permute-start(bf16[2,2,512,512]{3,2,1,0:T(8,128)(2,1)} %param.5), channel_id=1, source_target_pairs={{0,32},{32,64},{64,96},{96,128},{128,160},{160,192},{192,224},{224... | collective-permute-start | bytes 6291464 | tf_op jit(solution)/shard_map/ppermute | solution.py:14
  16.8 97.0 %collective-permute-start.1 = (bf16[2,2,512,512]{3,2,1,0:T(8,128)(2,1)}, bf16[2,2,512,512]{3,2,1,0:T(8,128)(2,1)}, u32[]{:S(2)}, u32[]{:S(2)}) collective-permute-start(bf16[2,2,512,512]{3,2,1,0:T(8,128)(2,1)} %param.5), channel_id=1, source_target_pairs={{32,0},{64,32},{96,64},{128,96},{160,128},{192,160},{224,192},{256... | collective-permute-start | bytes 6291464 | tf_op jit(solution)/shard_map/ppermute | solution.py:17
Sparse Core Ops, SparseCore 0:
  120.4 151.9 reduce-scatter.1
where the time goes:
time: 282 us; the launch traced here: 281 us
  waiting for transfers between devices  246 us (87%)
  between operations  14.7 us (5%)
  starting transfers between devices  12.2 us (4%)
  matrix products  6.46 us (2%)
    reduce_scatter x1, waiting for transfers between devices, local(): summed = lax.psum_scatter(acc, 'term', scatter_dimension=0, tiled=True)  152 us
    ppermute x1, waiting for transfers between devices, padded_2(): lax.ppermute(lax.slice_in_dim(block, block.shape[dim] - width, None, axis...  79.7 us
    ppermute x1, waiting for transfers between devices, padded_2(): lax.ppermute(lax.slice_in_dim(block, 0, width, axis=dim), axis, backward)  14 us
    ppermute x1, starting transfers between devices, padded_2(): lax.ppermute(lax.slice_in_dim(block, block.shape[dim] - width, None, axis...  10.2 us
    dot_general x1, matrix products, local(): jnp.einsum('asvc,sdc->asvd', inner, right_ops[0], preferred_element_type=...  6.46 us
  transfers between devices with their start and end apart: 3, of which 3 were waited for; matrix products, arithmetic and copies ran while one was open for 0% of the time, Pallas kernels for 0%

commit v1 on v0

v1 whole, which is shorter than its diff:
```python
import jax
import jax.numpy as jnp
from jax import lax
from jax.experimental import pallas as pl
from jax.experimental.pallas import tpu as pltpu
from jax.sharding import PartitionSpec as P

B = 512
V = 2
NX = 4
NZ = 4
RB = 16
CUT = 8
LAST = 15
MESH = pl.DeviceIdType.MESH
f32 = jnp.float32
bf16 = jnp.bfloat16


def kernel(
    shift_ref, live_ref, psi, left, right, out,
    lbuf, rbuf, win0, win1, acc0, acc1, cex0, cex1, pair0, pair1,
    xin0, xin1, xsum0, xsum1, zin0, zin1,
    load_sem, ysend, yrecv, esend, erecv, qsend, qrecv, fsend, frecv,
    csend, crecv, xsend, xrecv, zsend, zrecv,
):
    wins, accs, cexs, pairs = (win0, win1), (acc0, acc1), (cex0, cex1), (pair0, pair1)
    xins, xsums, zins = (xin0, xin1), (xsum0, xsum1), (zin0, zin1)
    sec, term = lax.axis_index("sec"), lax.axis_index("term")
    core = lax.rem(term, 2)
    chip = term // 2
    x = lax.rem(chip, NX)
    z = chip // NX

    def dev(s, zz, xx, cc):
        return (s, (zz * NX + xx) * 2 + cc)

    sibling = dev(sec, z, x, 1 - core)
    xpeer = [dev(sec, z, lax.rem(x + k, NX), core) for k in (1, 2, 3)]
    zpeer = [dev(sec, lax.rem(z + k, NZ), x, core) for k in (1, 2, 3)]
    has_low, has_high = sec > 0, sec < LAST
    cross_low, cross_high = sec == CUT, sec == CUT - 1
    low = dev(sec - 1, jnp.where(cross_low, NZ - 1 - z, z), x, core)
    high = dev(sec + 1, jnp.where(cross_high, NZ - 1 - z, z), x, core)

    loads = [
        pltpu.make_async_copy(psi.at[:, 0], win0.at[pl.ds(2, 2)], load_sem.at[0]),
        pltpu.make_async_copy(psi.at[:, 1], win1.at[pl.ds(2, 2)], load_sem.at[1]),
        pltpu.make_async_copy(left.at[0], lbuf, load_sem.at[2]),
        pltpu.make_async_copy(right.at[0], rbuf, load_sem.at[3]),
    ]
    for copy in loads:
        copy.start()

    barrier = pltpu.get_barrier_semaphore()
    for peer in [sibling] + xpeer + zpeer:
        pl.semaphore_signal(barrier, inc=1, device_id=peer, device_id_type=MESH)

    @pl.when(has_low)
    def _():
        pl.semaphore_signal(barrier, inc=1, device_id=low, device_id_type=MESH)

    @pl.when(has_high)
    def _():
        pl.semaphore_signal(barrier, inc=1, device_id=high, device_id_type=MESH)

    ends = jnp.where(has_low, 1, 0) + jnp.where(has_high, 1, 0)
    pl.semaphore_wait(barrier, 7 + ends)

    rows = pl.ds(pl.multiple_of(x * (B // NX), B // NX), B // NX)

    has = (has_low, has_high)
    cross = (cross_low, cross_high)
    direct = tuple(jnp.logical_and(h, jnp.logical_not(c)) for h, c in zip(has, cross))
    peer_of = (low, high)

    def remote(src, dst, ssem, rsem, device):
        return pltpu.make_async_remote_copy(
            src_ref=src, dst_ref=dst, send_sem=ssem, recv_sem=rsem, device_id=device, device_id_type=MESH
        )

    def halo_send(v, side):
        at = core + 4 * (1 - side)
        return remote(psi.at[core, v], wins[v].at[at], ysend.at[v, side], yrecv.at[v, 1 - side], peer_of[side])

    def entry_send(v, side):
        at = core + 4 * (1 - side)
        return remote(
            psi.at[core, v, rows], wins[v].at[at, rows], esend.at[v, side], erecv.at[v, 1 - side], peer_of[side]
        )

    def halo_recv(v, side):
        at = core + 4 * side
        return remote(psi.at[core, v], wins[v].at[at], ysend.at[v, side], yrecv.at[v, side], peer_of[side])

    def entry_recv(v, side):
        at = core + 4 * side
        return remote(
            psi.at[core, v, rows], wins[v].at[at, rows], esend.at[v, side], erecv.at[v, side], peer_of[side]
        )

    def quarter(v, side, k):
        at = core + 4 * side
        return remote(
            wins[v].at[at, rows], wins[v].at[at, rows], qsend.at[v, side, k], qrecv.at[v, side, k], xpeer[k]
        )

    def quarter_in(v, side, k):
        at = core + 4 * side
        whose = lax.rem(x + NX - 1 - k, NX)
        theirs = pl.ds(pl.multiple_of(whose * (B // NX), B // NX), B // NX)
        return remote(
            wins[v].at[at, theirs], wins[v].at[at, theirs], qsend.at[v, side, k], qrecv.at[v, side, k], xpeer[k]
        )

    def forward(v, side):
        at = core + 4 * side
        return remote(wins[v].at[at], wins[v].at[at], fsend.at[v, side], frecv.at[v, side], sibling)

    def forward_in(v, side):
        at = 1 - core + 4 * side
        return remote(wins[v].at[at], wins[v].at[at], fsend.at[v, side], frecv.at[v, side], sibling)

    def start_halo(v):
        for side in (0, 1):
            @pl.when(direct[side])
            def _():
                halo_send(v, side).start()

            @pl.when(cross[side])
            def _():
                entry_send(v, side).start()

    def sent_halo(v):
        for side in (0, 1):
            @pl.when(direct[side])
            def _():
                halo_send(v, side).wait_send()

            @pl.when(cross[side])
            def _():
                entry_send(v, side).wait_send()

    def pass_halo(v):
        for side in (0, 1):
            @pl.when(cross[side])
            def _():
                entry_recv(v, side).wait_recv()
                for k in range(3):
                    quarter(v, side, k).start()

        for side in (0, 1):
            @pl.when(direct[side])
            def _():
                halo_recv(v, side).wait_recv()
                forward(v, side).start()

        for side in (0, 1):
            @pl.when(cross[side])
            def _():
                for k in range(3):
                    quarter_in(v, side, k).wait_recv()
                forward(v, side).start()

    def finish_halo(v):
        for side in (0, 1):
            @pl.when(has[side])
            def _():
                forward_in(v, side).wait_recv()

    def drain_halo(v):
        for side in (0, 1):
            @pl.when(has[side])
            def _():
                forward(v, side).wait_send()

            @pl.when(cross[side])
            def _():
                for k in range(3):
                    quarter(v, side, k).wait_send()

    def exchange(v, s):
        return remote(
            accs[v].at[s, :, 1 - core], cexs[v].at[s], csend.at[v, s], crecv.at[v, s], sibling
        )

    def xsend_of(v, s, k):
        return remote(
            pairs[v].at[s, :, lax.rem(x + 1 + k, NX)], xins[v].at[s, k],
            xsend.at[v, s, k], xrecv.at[v, s, k], xpeer[k],
        )

    def zsend_of(v, s, k):
        return remote(
            xsums[v].at[s, lax.rem(z + 1 + k, NZ)], zins[v].at[s, k],
            zsend.at[v, s, k], zrecv.at[v, s, k], zpeer[k],
        )

    def compute(v, s):
        block = wins[v][s + 2 - shift_ref[0]]
        inner = jnp.dot(lbuf[s], block, preferred_element_type=f32).astype(bf16)
        outer = lax.dot_general(inner, rbuf[s], (((1,), (1,)), ((), ())), preferred_element_type=f32)
        outer = outer * live_ref[0].astype(f32)
        accs[v][s] = outer.astype(bf16).reshape(NX * NZ, 2, RB, B)

    start_halo(0)
    for side in (0, 1):
        @pl.when(jnp.logical_not(has[side]))
        def _():
            for v in range(V):
                for at in range(2):
                    wins[v][4 * side + at] = jnp.zeros((B, B), bf16)

    for copy in loads:
        copy.wait()

    for v in range(V):
        pass_halo(v)
        sent_halo(v)
        if v + 1 < V:
            start_halo(v + 1)
        finish_halo(v)
        for s in range(2):
            compute(v, s)
            exchange(v, s).start()
        for s in range(2):
            exchange(v, s).wait_recv()
            both = accs[v][s, :, core].astype(f32) + cexs[v][s].astype(f32)
            pairs[v][s] = both.astype(bf16).reshape(NZ, NX, RB, B)
            for k in range(3):
                xsend_of(v, s, k).start()
        for s in range(2):
            total = pairs[v][s, :, x].astype(f32)
            for k in range(3):
                xsend_of(v, s, k).wait_recv()
                total += xins[v][s, k].astype(f32)
            xsums[v][s] = total.astype(bf16)
            for k in range(3):
                zsend_of(v, s, k).start()
        for s in range(2):
            total = xsums[v][s, z].astype(f32)
            for k in range(3):
                zsend_of(v, s, k).wait_recv()
                total += zins[v][s, k].astype(f32)
            out[s, v] = total.astype(bf16)

    for v in range(V):
        drain_halo(v)
        for s in range(2):
            exchange(v, s).wait_send()
            for k in range(3):
                xsend_of(v, s, k).wait_send()
                zsend_of(v, s, k).wait_send()


def local(psi, left_ops, right_ops, shift, live):
    dma = pltpu.SemaphoreType.DMA
    pairs_of = lambda shape: [pltpu.VMEM(shape, bf16)] * V
    hbm = pl.BlockSpec(memory_space=pl.ANY)
    smem = pl.BlockSpec(memory_space=pltpu.SMEM)
    return pl.pallas_call(
        kernel,
        out_shape=jax.ShapeDtypeStruct((2, V, RB, B), bf16),
        in_specs=[smem, smem, hbm, hbm, hbm],
        out_specs=pl.BlockSpec(memory_space=pltpu.VMEM),
        scratch_shapes=[pltpu.VMEM((2, B, B), bf16)] * 2
        + pairs_of((6, B, B))
        + pairs_of((2, NX * NZ, 2, RB, B))
        + pairs_of((2, NX * NZ, RB, B))
        + pairs_of((2, NZ, NX, RB, B))
        + pairs_of((2, 3, NZ, RB, B))
        + pairs_of((2, NZ, RB, B))
        + pairs_of((2, 3, RB, B))
        + [dma((4,))]
        + [dma((V, 2))] * 4
        + [dma((V, 2, 3))] * 2
        + [dma((V, 2))] * 2
        + [dma((V, 2))] * 2
        + [dma((V, 2, 3))] * 4,
        compiler_params=pltpu.CompilerParams(
            collective_id=0, has_side_effects=True, vmem_limit_bytes=40 * 2**20
        ),
        name="sigma",
    )(shift, live, psi, left_ops, right_ops)


def solution(mesh):
    in_specs = (
        P("sec", None, None, None),
        P("term", "sec", None, None),
        P("term", "sec", None, None),
        P("term"),
        P("term"),
    )
    out_specs = P("sec", None, "term", None)
    return jax.shard_map(local, mesh=mesh, in_specs=in_specs, out_specs=out_specs, check_vma=False)
```

time: 282 us -> 69.8 us (0.25)
  waiting for transfers between devices: 246 us -> 0 us
  Pallas kernels: 0 us -> 63.6 us
  between operations: 14.7 us -> 1.32 us
  starting transfers between devices: 12.2 us -> 0 us
  matrix products: 6.46 us -> 0 us
  local copies, waits for them, and re-layouts: 0.01 us -> 4.66 us
    reduce_scatter x1 -> x0, waiting for transfers between devices: 152 us -> none  [local(): summed = lax.psum_scatter(acc, 'term', scatter_dimension=0, tiled=True)]
    ppermute x2 -> x0, waiting for transfers between devices: 93.7 us -> none  [the longest x1 79.7 us: padded_2(): lax.ppermute(lax.slice_in_dim(block, block.shape[dim] - width, None, axis...]
    pallas_call x0 -> x1, Pallas kernels: none -> 63.6 us  [local(): pl.pallas_call(kernel, out_shape=jax.ShapeDtypeStruct((2, V, RB, B), bf16...]
    ppermute x2 -> x0, starting transfers between devices: 12.2 us -> none  [the longest x1 10.2 us: padded_2(): lax.ppermute(lax.slice_in_dim(block, block.shape[dim] - width, None, axis...]
    dot_general x1 -> x0, matrix products: 6.46 us -> none  [local(): jnp.einsum('asvc,sdc->asvd', inner, right_ops[0], preferred_element_type=...]
    unnamed x2 -> x7, local copies, waits for them, and re-layouts: 0.01 us -> 4.66 us
  transfers between devices with their start and end apart: 3 -> 0, of which waited for: 3 -> 0; matrix products, arithmetic and copies ran while one was open for 0% -> 0% of each run, Pallas kernels for 0% -> 0%
where the time goes in v1:
time: 69.8 us; the launch traced here: 69.6 us
  Pallas kernels  63.6 us (91%)
  local copies, waits for them, and re-layouts  4.66 us (7%)
  between operations  1.32 us (2%)
    pallas_call x1, Pallas kernels, local(): pl.pallas_call(kernel, out_shape=jax.ShapeDtypeStruct((2, V, RB, B), bf16...  63.6 us
    unnamed x7, local copies, waits for them, and re-layouts  4.66 us

profile of v1, /device:TPU:56, one launch (start us, length us, event | category | flops | bytes accessed | tf_op | source)
XLA Modules:
  0.0 69.6 jit_solution(1238426855192386508)
XLA Ops:
  1.3 0.0 copy-start
  1.3 1.6 %copy-done = bf16[2,2,512,512]{3,2,1,0:T(8,128)(2,1)S(1)} copy-done((bf16[2,2,512,512]{3,2,1,0:T(8,128)(2,1)S(1)}, bf16[2,2,512,512]{3,2,1,0:T(8,128)(2,1)}, u32[]{:S(2)}) %copy-start) | copy-done | bytes 2097176
  2.9 0.0 copy-start.1
  2.9 1.2 %copy-done.1 = bf16[1,2,512,512]{3,2,1,0:T(8,128)(2,1)S(1)} copy-done((bf16[1,2,512,512]{3,2,1,0:T(8,128)(2,1)S(1)}, bf16[1,2,512,512]{3,2,1,0:T(8,128)(2,1)}, u32[]{:S(2)}) %copy-start.1) | copy-done | bytes 1048600
  4.1 0.0 copy-start.2
  4.1 1.2 %copy-done.2 = bf16[1,2,512,512]{3,2,1,0:T(8,128)(2,1)S(1)} copy-done((bf16[1,2,512,512]{3,2,1,0:T(8,128)(2,1)S(1)}, bf16[1,2,512,512]{3,2,1,0:T(8,128)(2,1)}, u32[]{:S(2)}) %copy-start.2) | copy-done | bytes 1048600
  5.3 63.6 %sigma.1 = bf16[2,2,16,512]{3,2,1,0:T(8,128)(2,1)S(1)} custom-call(s32[1]{0:T(128)S(6)} %copy.7.shift_ref, s32[1]{0:T(128)S(6)} %copy.8.live_ref, bf16[2,2,512,512]{3,2,1,0:T(8,128)(2,1)S(1)} %copy-done, bf16[1,2,512,512]{3,2,1,0:T(8,128)(2,1)S(1)} %copy-done.1, bf16[1,2,512,512]{3,2,1,0:T(8,128)(2,1)S(1)} %copy-done.2), custom_call_target="tpu_custom_call" | custom-call | tf_op jit(solution)/shard_map/sigma/pallas_call | solution.py:261
  69.0 0.6 copy.9
Async XLA Ops:
  1.3 1.6 %copy-start = (bf16[2,2,512,512]{3,2,1,0:T(8,128)(2,1)S(1)}, bf16[2,2,512,512]{3,2,1,0:T(8,128)(2,1)}, u32[]{:S(2)}) copy-start(bf16[2,2,512,512]{3,2,1,0:T(8,128)(2,1)} %psi.1) | copy-start | bytes 6291460
  2.9 1.2 %copy-start.1 = (bf16[1,2,512,512]{3,2,1,0:T(8,128)(2,1)S(1)}, bf16[1,2,512,512]{3,2,1,0:T(8,128)(2,1)}, u32[]{:S(2)}) copy-start(bf16[1,2,512,512]{3,2,1,0:T(8,128)(2,1)} %left.1) | copy-start | bytes 3145732
  4.1 1.2 %copy-start.2 = (bf16[1,2,512,512]{3,2,1,0:T(8,128)(2,1)S(1)}, bf16[1,2,512,512]{3,2,1,0:T(8,128)(2,1)}, u32[]{:S(2)}) copy-start(bf16[1,2,512,512]{3,2,1,0:T(8,128)(2,1)} %right.1) | copy-start | bytes 3145732

commit v2 on v0

v2 whole, which is shorter than its diff:
```python
import jax
import jax.numpy as jnp
from jax import lax
from jax.experimental import pallas as pl
from jax.experimental.pallas import tpu as pltpu
from jax.sharding import PartitionSpec as P

B = 512
V = 2
NX = 4
NZ = 4
RB = 16
QR = B // NX
NF = 192
HF = NF // 2
ND = B - 2 * NF
VMEM_LIMIT = 60 * 2**20
CUT = 8
LAST = 15
MESH = pl.DeviceIdType.MESH
HALO, COMP, RS = 1, 1, 3
f32 = jnp.float32
bf16 = jnp.bfloat16


def kernel(
    shift_ref, live_ref, psi, left, right, out,
    lbuf, rbuf, win0, win1, acc0, acc1, cex0, cex1, pair0, pair1,
    xin0, xin1, xsum0, xsum1, zin0, zin1,
    load_sem, ysend, yrecv, hsend, hrecv, esend, erecv, qsend, qrecv,
    fsend, frecv, csend, crecv, xsend, xrecv, zsend, zrecv,
):
    wins, accs, cexs, pairs = (win0, win1), (acc0, acc1), (cex0, cex1), (pair0, pair1)
    xins, xsums, zins = (xin0, xin1), (xsum0, xsum1), (zin0, zin1)
    sec, term = lax.axis_index("sec"), lax.axis_index("term")
    core = lax.rem(term, 2)
    chip = term // 2
    x = lax.rem(chip, NX)
    z = chip // NX
    xa = (lax.rem(x + NX - 1, NX), lax.rem(x + 1, NX))

    def dev(s, zz, xx, cc):
        return (s, (zz * NX + xx) * 2 + cc)

    sibling = dev(sec, z, x, 1 - core)
    xpeer = [dev(sec, z, xx, core) for xx in xa]
    xring = [dev(sec, z, lax.rem(x + k, NX), core) for k in (1, 2, 3)]
    zpeer = [dev(sec, lax.rem(z + k, NZ), x, core) for k in (1, 2, 3)]
    has = (sec > 0, sec < LAST)
    cross = (sec == CUT, sec == CUT - 1)
    direct = tuple(jnp.logical_and(h, jnp.logical_not(c)) for h, c in zip(has, cross))
    ypeer = (
        dev(sec - 1, jnp.where(cross[0], NZ - 1 - z, z), x, core),
        dev(sec + 1, jnp.where(cross[1], NZ - 1 - z, z), x, core),
    )

    loads = [
        pltpu.make_async_copy(psi.at[:, 0], win0.at[pl.ds(2, 2)], load_sem.at[0]),
        pltpu.make_async_copy(psi.at[:, 1], win1.at[pl.ds(2, 2)], load_sem.at[1]),
        pltpu.make_async_copy(left.at[0], lbuf, load_sem.at[2]),
        pltpu.make_async_copy(right.at[0], rbuf, load_sem.at[3]),
    ]
    for copy in loads:
        copy.start()

    barrier = pltpu.get_barrier_semaphore()
    for peer in [sibling] + xring + zpeer:
        pl.semaphore_signal(barrier, inc=1, device_id=peer, device_id_type=MESH)
    for side in (0, 1):
        @pl.when(has[side])
        def _():
            pl.semaphore_signal(barrier, inc=1, device_id=ypeer[side], device_id_type=MESH)

    ends = jnp.where(has[0], 1, 0) + jnp.where(has[1], 1, 0)
    pl.semaphore_wait(barrier, 7 + ends)

    def remote(src, dst, ssem, rsem, device):
        return pltpu.make_async_remote_copy(
            src_ref=src, dst_ref=dst, send_sem=ssem, recv_sem=rsem, device_id=device, device_id_type=MESH
        )

    odd = lax.rem(x, 2)

    def block_rows(n):
        return pl.ds(pl.multiple_of(n * QR, QR), QR)

    def shared_rows(parity, q):
        return pl.ds(pl.multiple_of(parity * NF + q * HF, HF), HF)

    def y_rows(side, j):
        return pl.ds(2 * NF, ND) if j == 2 else shared_rows(odd, j ^ side)

    def spot(side):
        return core + 4 * side

    def y_copy(v, side, j, landing):
        at = side if landing else 1 - side
        part = y_rows(at, j)
        return remote(
            psi.at[core, v, part], wins[v].at[spot(at), part], ysend.at[v, side, j], yrecv.at[v, at, j], ypeer[side]
        )

    def h_copy(v, side, q, landing):
        part = shared_rows(1 - odd, q) if landing else shared_rows(odd, q)
        place = wins[v].at[spot(side), part]
        return remote(place, place, hsend.at[v, side, q], hrecv.at[v, side, q], xpeer[q])

    def e_copy(v, side, landing):
        at = side if landing else 1 - side
        part = block_rows(x)
        return remote(
            psi.at[core, v, part], wins[v].at[spot(at), part], esend.at[v, side], erecv.at[v, at], ypeer[side]
        )

    def q_copy(v, side, k, landing):
        place = wins[v].at[spot(side), block_rows(lax.rem(x + 3 - k, NX) if landing else x)]
        return remote(place, place, qsend.at[v, side, k], qrecv.at[v, side, k], xring[k])

    def pass_on(v, side, part, n):
        place = wins[v].at[spot(side), part]
        return remote(place, place, fsend.at[v, side, n], frecv.at[v, side], sibling)

    def passed(v, side):
        place = wins[v].at[1 - core + 4 * side]
        return remote(place, place, fsend.at[v, side, 0], frecv.at[v, side], sibling)

    def issue_y(v, j):
        if j == 2 and not ND:
            return
        for side in (0, 1):
            @pl.when(direct[side])
            def _():
                y_copy(v, side, j, False).start()

    def issue_e(v):
        for side in (0, 1):
            @pl.when(cross[side])
            def _():
                e_copy(v, side, False).start()

    def pass_y(v, j):
        if j == 2 and not ND:
            return
        for side in (0, 1):
            @pl.when(direct[side])
            def _():
                y_copy(v, side, j, True).wait_recv()
                if j < 2:
                    h_copy(v, side, j ^ side, False).start()
                pass_on(v, side, y_rows(side, j), j).start()

    def pass_x(v, j):
        for side in (0, 1):
            @pl.when(direct[side])
            def _():
                h_copy(v, side, j ^ side, True).wait_recv()
                pass_on(v, side, shared_rows(1 - odd, j ^ side), 3 + j).start()

    def pass_e(v):
        for side in (0, 1):
            @pl.when(cross[side])
            def _():
                e_copy(v, side, True).wait_recv()
                for k in range(3):
                    q_copy(v, side, k, False).start()
                pass_on(v, side, block_rows(x), 0).start()

    def pass_q(v):
        for side in (0, 1):
            @pl.when(cross[side])
            def _():
                for k in (0, 2, 1):
                    q_copy(v, side, k, True).wait_recv()
                    pass_on(v, side, block_rows(lax.rem(x + 3 - k, NX)), 1 + k).start()

    def finish(v):
        for side in (0, 1):
            @pl.when(has[side])
            def _():
                passed(v, side).wait_recv()

    def drain(v):
        for side in (0, 1):
            @pl.when(direct[side])
            def _():
                for j in (0, 1, 2):
                    if j < 2 or ND:
                        y_copy(v, side, j, False).wait_send()
                        pass_on(v, side, y_rows(side, j), j).wait_send()
                for j in (0, 1):
                    h_copy(v, side, j, False).wait_send()
                    pass_on(v, side, shared_rows(0, 0), 3 + j).wait_send()

            @pl.when(cross[side])
            def _():
                e_copy(v, side, False).wait_send()
                for k in range(3):
                    q_copy(v, side, k, False).wait_send()
                for n in range(4):
                    pass_on(v, side, block_rows(0), n).wait_send()

    def exchange(v, s):
        return remote(accs[v].at[s, :, 1 - core], cexs[v].at[s], csend.at[v, s], crecv.at[v, s], sibling)

    def xhop(v, s, k):
        return remote(
            pairs[v].at[s, :, lax.rem(x + 1 + k, NX)], xins[v].at[s, k], xsend.at[v, s, k], xrecv.at[v, s, k], xring[k]
        )

    def zhop(v, s, k):
        return remote(
            xsums[v].at[s, lax.rem(z + 1 + k, NZ)], zins[v].at[s, k], zsend.at[v, s, k], zrecv.at[v, s, k], zpeer[k]
        )

    def compute(v, s):
        block = wins[v][s + 2 - shift_ref[0]]
        inner = jnp.dot(lbuf[s], block, preferred_element_type=f32).astype(bf16)
        outer = lax.dot_general(inner, rbuf[s], (((1,), (1,)), ((), ())), preferred_element_type=f32)
        outer = outer * live_ref[0].astype(f32)
        accs[v][s] = outer.astype(bf16).reshape(NX * NZ, 2, RB, B)

    def products(v):
        for s in range(2):
            if COMP:
                compute(v, s)
            if RS >= 1:
                exchange(v, s).start()

    def add_cores(v):
        for s in range(2 if RS >= 1 else 0):
            exchange(v, s).wait_recv()
            both = accs[v][s, :, core].astype(f32) + cexs[v][s].astype(f32)
            pairs[v][s] = both.astype(bf16).reshape(NZ, NX, RB, B)
            if RS >= 2:
                for k in range(3):
                    xhop(v, s, k).start()

    def add_x(v):
        for s in range(2 if RS >= 2 else 0):
            total = pairs[v][s, :, x].astype(f32)
            for k in range(3):
                xhop(v, s, k).wait_recv()
                total += xins[v][s, k].astype(f32)
            xsums[v][s] = total.astype(bf16)
            if RS >= 3:
                for k in range(3):
                    zhop(v, s, k).start()

    def add_z(v):
        for s in range(2 if RS >= 3 else 0):
            total = xsums[v][s, z].astype(f32)
            for k in range(3):
                zhop(v, s, k).wait_recv()
                total += zins[v][s, k].astype(f32)
            out[s, v] = total.astype(bf16)

    if HALO:
        issue_y(0, 0)
        issue_e(0)
        issue_y(0, 1)
    for side in (0, 1):
        @pl.when(jnp.logical_not(has[side]))
        def _():
            for v in range(V):
                for at in range(2):
                    wins[v][4 * side + at] = jnp.zeros((B, B), bf16)

    for copy in loads:
        copy.wait()

    at_cut = jnp.logical_or(cross[0], cross[1])
    if HALO:
        pass_y(0, 0)
        issue_y(0, 2)
        if not ND:
            issue_y(1, 0)
        pass_y(0, 1)
        if ND:
            issue_y(1, 0)
        else:
            issue_y(1, 1)
        pass_e(0)
        issue_e(1)
        pass_x(0, 0)
        pass_y(0, 2)
        if ND:
            issue_y(1, 1)
        pass_x(0, 1)
        pass_y(1, 0)
        issue_y(1, 2)

        @pl.when(at_cut)
        def _():
            pass_y(1, 1)
            pass_e(1)
            pass_q(0)

        finish(0)
    products(0)
    if HALO:
        @pl.when(jnp.logical_not(at_cut))
        def _():
            pass_y(1, 1)

    add_cores(0)
    if HALO:
        pass_x(1, 0)
        pass_y(1, 2)
        pass_x(1, 1)
        pass_q(1)
        finish(1)
    products(1)
    add_x(0)
    add_cores(1)
    add_z(0)
    add_x(1)
    add_z(1)

    for v in range(V):
        if HALO:
            drain(v)
        for s in range(2):
            if RS >= 1:
                exchange(v, s).wait_send()
            if RS >= 2:
                for k in range(3):
                    xhop(v, s, k).wait_send()
            if RS >= 3:
                for k in range(3):
                    zhop(v, s, k).wait_send()


def local(psi, left_ops, right_ops, shift, live):
    dma = pltpu.SemaphoreType.DMA
    per_vector = lambda shape: [pltpu.VMEM(shape, bf16)] * V
    hbm = pl.BlockSpec(memory_space=pltpu.HBM)
    smem = pl.BlockSpec(memory_space=pltpu.SMEM)
    return pl.pallas_call(
        kernel,
        out_shape=jax.ShapeDtypeStruct((2, V, RB, B), bf16),
        in_specs=[smem, smem, hbm, hbm, hbm],
        out_specs=pl.BlockSpec(memory_space=pltpu.VMEM),
        scratch_shapes=[pltpu.VMEM((2, B, B), bf16)] * 2
        + per_vector((6, B, B))
        + per_vector((2, NX * NZ, 2, RB, B))
        + per_vector((2, NX * NZ, RB, B))
        + per_vector((2, NZ, NX, RB, B))
        + per_vector((2, 3, NZ, RB, B))
        + per_vector((2, NZ, RB, B))
        + per_vector((2, 3, RB, B))
        + [dma((4,))]
        + [dma((V, 2, 3))] * 2
        + [dma((V, 2, 2))] * 2
        + [dma((V, 2))] * 2
        + [dma((V, 2, 3))] * 2
        + [dma((V, 2, 5)), dma((V, 2))]
        + [dma((V, 2))] * 2
        + [dma((V, 2, 3))] * 4,
        compiler_params=pltpu.CompilerParams(
            collective_id=0, has_side_effects=True, vmem_limit_bytes=VMEM_LIMIT
        ),
        name="sigma",
    )(shift, live, psi, left_ops, right_ops)


def solution(mesh):
    in_specs = (
        P("sec", None, None, None),
        P("term", "sec", None, None),
        P("term", "sec", None, None),
        P("term"),
        P("term"),
    )
    out_specs = P("sec", None, "term", None)
    return jax.shard_map(local, mesh=mesh, in_specs=in_specs, out_specs=out_specs, check_vma=False)
```

time: 282 us -> 54.6 us (0.19)
  waiting for transfers between devices: 246 us -> 0 us
  Pallas kernels: 0 us -> 51.6 us
  between operations: 14.7 us -> 1.3 us
  starting transfers between devices: 12.2 us -> 0 us
  matrix products: 6.46 us -> 0 us
    reduce_scatter x1 -> x0, waiting for transfers between devices: 152 us -> none  [local(): summed = lax.psum_scatter(acc, 'term', scatter_dimension=0, tiled=True)]
    ppermute x2 -> x0, waiting for transfers between devices: 93.7 us -> none  [the longest x1 79.7 us: padded_2(): lax.ppermute(lax.slice_in_dim(block, block.shape[dim] - width, None, axis...]
    pallas_call x0 -> x1, Pallas kernels: none -> 51.6 us  [local(): pl.pallas_call(kernel, out_shape=jax.ShapeDtypeStruct((2, V, RB, B), bf16...]
    ppermute x2 -> x0, starting transfers between devices: 12.2 us -> none  [the longest x1 10.2 us: padded_2(): lax.ppermute(lax.slice_in_dim(block, block.shape[dim] - width, None, axis...]
    dot_general x1 -> x0, matrix products: 6.46 us -> none  [local(): jnp.einsum('asvc,sdc->asvd', inner, right_ops[0], preferred_element_type=...]
  transfers between devices with their start and end apart: 3 -> 0, of which waited for: 3 -> 0; matrix products, arithmetic and copies ran while one was open for 0% -> 0% of each run, Pallas kernels for 0% -> 0%
where the time goes in v2:
time: 54.6 us; the launch traced here: 54.4 us
  Pallas kernels  51.6 us (95%)
  local copies, waits for them, and re-layouts  1.47 us (3%)
  between operations  1.3 us (2%)
    pallas_call x1, Pallas kernels, local(): pl.pallas_call(kernel, out_shape=jax.ShapeDtypeStruct((2, V, RB, B), bf16...  51.6 us
    unnamed x1, local copies, waits for them, and re-layouts  1.47 us

profile of v2, /device:TPU:56, one launch (start us, length us, event | category | flops | bytes accessed | tf_op | source)
XLA Modules:
  0.0 54.4 jit_solution(9041184785681264166)
XLA Ops:
  1.3 51.6 %sigma.1 = bf16[2,2,16,512]{3,2,1,0:T(8,128)(2,1)} custom-call(s32[1]{0:T(128)S(6)} %copy.7.shift_ref, s32[1]{0:T(128)S(6)} %copy.8.live_ref, bf16[2,2,512,512]{3,2,1,0:T(8,128)(2,1)} %psi.1, bf16[1,2,512,512]{3,2,1,0:T(8,128)(2,1)} %left.1, bf16[1,2,512,512]{3,2,1,0:T(8,128)(2,1)} %right.1), custom_call_target="tpu_custom_call" | custom-call | tf_op jit(solution)/shard_map/sigma/pallas_call | solution.py:338
  52.9 1.5 %copy.9 = bf16[2,2,16,512]{3,2,1,0:T(8,128)(2,1)} copy(bf16[2,2,16,512]{3,2,1,0:T(8,128)(2,1)} %sigma.1) | data formatting | bytes 131072

commit v3 on v2

--- a/solution.py
+++ b/solution.py
@@ -11,10 +11,11 @@
 NZ = 4
 RB = 16
 QR = B // NX
-NF = 192
+QH = QR // 2
+NF = 128
 HF = NF // 2
 ND = B - 2 * NF
-VMEM_LIMIT = 60 * 2**20
+VMEM_LIMIT = 53 * 2**20 + 2**19
 CUT = 8
 LAST = 15
 MESH = pl.DeviceIdType.MESH
@@ -105,16 +106,19 @@
         place = wins[v].at[spot(side), part]
         return remote(place, place, hsend.at[v, side, q], hrecv.at[v, side, q], xpeer[q])
 
-    def e_copy(v, side, landing):
+    def piece_rows(n, h):
+        return pl.ds(pl.multiple_of(n * QR + h * QH, QH), QH)
+
+    def e_copy(v, side, h, landing):
         at = side if landing else 1 - side
-        part = block_rows(x)
+        part = piece_rows(x, h)
         return remote(
-            psi.at[core, v, part], wins[v].at[spot(at), part], esend.at[v, side], erecv.at[v, at], ypeer[side]
-        )
-
-    def q_copy(v, side, k, landing):
-        place = wins[v].at[spot(side), block_rows(lax.rem(x + 3 - k, NX) if landing else x)]
-        return remote(place, place, qsend.at[v, side, k], qrecv.at[v, side, k], xring[k])
+            psi.at[core, v, part], wins[v].at[spot(at), part], esend.at[v, side, h], erecv.at[v, at, h], ypeer[side]
+        )
+
+    def q_copy(v, side, h, k, landing):
+        place = wins[v].at[spot(side), piece_rows(lax.rem(x + 3 - k, NX) if landing else x, h)]
+        return remote(place, place, qsend.at[v, side, 3 * h + k], qrecv.at[v, side, 3 * h + k], xring[k])
 
     def pass_on(v, side, part, n):
         place = wins[v].at[spot(side), part]
@@ -132,11 +136,11 @@
             def _():
                 y_copy(v, side, j, False).start()
 
-    def issue_e(v):
+    def issue_e(v, h):
         for side in (0, 1):
             @pl.when(cross[side])
             def _():
-                e_copy(v, side, False).start()
+                e_copy(v, side, h, False).start()
 
     def pass_y(v, j):
         if j == 2 and not ND:
@@ -156,21 +160,23 @@
                 h_copy(v, side, j ^ side, True).wait_recv()
                 pass_on(v, side, shared_rows(1 - odd, j ^ side), 3 + j).start()
 
-    def pass_e(v):
+    def pass_e(v, h):
         for side in (0, 1):
             @pl.when(cross[side])
             def _():
-                e_copy(v, side, True).wait_recv()
-                for k in range(3):
-                    q_copy(v, side, k, False).start()
-                pass_on(v, side, block_rows(x), 0).start()
+                e_copy(v, side, h, True).wait_recv()
+                for k in range(3):
+                    q_copy(v, side, h, k, False).start()
+                if h == 1:
+                    pass_on(v, side, block_rows(x), 0).start()
 
     def pass_q(v):
         for side in (0, 1):
             @pl.when(cross[side])
             def _():
                 for k in (0, 2, 1):
-                    q_copy(v, side, k, True).wait_recv()
+                    for h in (0, 1):
+                        q_copy(v, side, h, k, True).wait_recv()
                     pass_on(v, side, block_rows(lax.rem(x + 3 - k, NX)), 1 + k).start()
 
     def finish(v):
@@ -193,9 +199,10 @@
 
             @pl.when(cross[side])
             def _():
-                e_copy(v, side, False).wait_send()
-                for k in range(3):
-                    q_copy(v, side, k, False).wait_send()
+                for h in (0, 1):
+                    e_copy(v, side, h, False).wait_send()
+                    for k in range(3):
+                        q_copy(v, side, h, k, False).wait_send()
                 for n in range(4):
                     pass_on(v, side, block_rows(0), n).wait_send()
 
@@ -256,8 +263,10 @@
 
     if HALO:
         issue_y(0, 0)
-        issue_e(0)
+        issue_e(0, 0)
         issue_y(0, 1)
+        issue_e(0, 1)
+        issue_y(0, 2)
     for side in (0, 1):
         @pl.when(jnp.logical_not(has[side]))
         def _():
@@ -271,28 +280,24 @@
     at_cut = jnp.logical_or(cross[0], cross[1])
     if HALO:
         pass_y(0, 0)
-        issue_y(0, 2)
-        if not ND:
-            issue_y(1, 0)
+        issue_y(1, 0)
+        pass_e(0, 0)
+        issue_e(1, 0)
         pass_y(0, 1)
-        if ND:
-            issue_y(1, 0)
-        else:
-            issue_y(1, 1)
-        pass_e(0)
-        issue_e(1)
+        issue_y(1, 1)
+        pass_e(0, 1)
+        issue_e(1, 1)
         pass_x(0, 0)
         pass_y(0, 2)
-        if ND:
-            issue_y(1, 1)
+        issue_y(1, 2)
+        pass_e(1, 0)
         pass_x(0, 1)
         pass_y(1, 0)
-        issue_y(1, 2)
 
         @pl.when(at_cut)
         def _():
+            pass_e(1, 1)
             pass_y(1, 1)
-            pass_e(1)
             pass_q(0)
 
         finish(0)
@@ -310,8 +315,8 @@
         pass_q(1)
         finish(1)
     products(1)
+    add_cores(1)
     add_x(0)
-    add_cores(1)
     add_z(0)
     add_x(1)
     add_z(1)
@@ -351,8 +356,8 @@
         + [dma((4,))]
         + [dma((V, 2, 3))] * 2
         + [dma((V, 2, 2))] * 2
-        + [dma((V, 2))] * 2
-        + [dma((V, 2, 3))] * 2
+        + [dma((V, 2, 2))] * 2
+        + [dma((V, 2, 6))] * 2
         + [dma((V, 2, 5)), dma((V, 2))]
         + [dma((V, 2))] * 2
         + [dma((V, 2, 3))] * 4,

time: 54.6 us -> 50.4 us (0.923)
  Pallas kernels: 51.6 us -> 48.3 us
  local copies, waits for them, and re-layouts: 1.47 us -> 0.63 us
    pallas_call x1, Pallas kernels: 51.6 us -> 48.3 us  [local(): pl.pallas_call(kernel, out_shape=jax.ShapeDtypeStruct((2, V, RB, B), bf16...]
    unnamed x1, local copies, waits for them, and re-layouts: 1.47 us -> 0.63 us
where the time goes in v3:
time: 50.4 us; the launch traced here: 50.3 us
  Pallas kernels  48.3 us (96%)
  between operations  1.3 us (3%)
  local copies, waits for them, and re-layouts  0.63 us (1%)
    pallas_call x1, Pallas kernels, local(): pl.pallas_call(kernel, out_shape=jax.ShapeDtypeStruct((2, V, RB, B), bf16...  48.3 us

profile of v3, /device:TPU:56, one launch (start us, length us, event | category | flops | bytes accessed | tf_op | source)
XLA Modules:
  0.0 50.3 jit_solution(9005741105459216923)
XLA Ops:
  1.3 48.3 %sigma.1 = bf16[2,2,16,512]{3,2,1,0:T(8,128)(2,1)S(1)} custom-call(s32[1]{0:T(128)S(6)} %copy.7.shift_ref, s32[1]{0:T(128)S(6)} %copy.8.live_ref, bf16[2,2,512,512]{3,2,1,0:T(8,128)(2,1)} %psi.1, bf16[1,2,512,512]{3,2,1,0:T(8,128)(2,1)} %left.1, bf16[1,2,512,512]{3,2,1,0:T(8,128)(2,1)} %right.1), custom_call_target="tpu_custom_call" | custom-call | tf_op jit(solution)/shard_map/sigma/pallas_call | solution.py:343
  49.6 0.6 %copy.9 = bf16[2,2,16,512]{3,2,1,0:T(8,128)(2,1)} copy(bf16[2,2,16,512]{3,2,1,0:T(8,128)(2,1)S(1)} %sigma.1) | data formatting | bytes 131072

commit v4 on v3

--- a/solution.py
+++ b/solution.py
@@ -19,20 +19,20 @@
 CUT = 8
 LAST = 15
 MESH = pl.DeviceIdType.MESH
-HALO, COMP, RS = 1, 1, 3
 f32 = jnp.float32
 bf16 = jnp.bfloat16
 
 
 def kernel(
     shift_ref, live_ref, psi, left, right, out,
-    lbuf, rbuf, win0, win1, acc0, acc1, cex0, cex1, pair0, pair1,
+    lbuf, rbuf, rbuf0, rbuf1, win0, win1, acc0, acc1, cex0, cex1, pair0, pair1,
     xin0, xin1, xsum0, xsum1, zin0, zin1,
-    load_sem, ysend, yrecv, hsend, hrecv, esend, erecv, qsend, qrecv,
+    load_sem, ysend, yrecv, hsend, hrecv, esend, erecv, rsend, rrecv, qsend, qrecv,
     fsend, frecv, csend, crecv, xsend, xrecv, zsend, zrecv,
 ):
     wins, accs, cexs, pairs = (win0, win1), (acc0, acc1), (cex0, cex1), (pair0, pair1)
     xins, xsums, zins = (xin0, xin1), (xsum0, xsum1), (zin0, zin1)
+    rbufs = (rbuf0, rbuf1)
     sec, term = lax.axis_index("sec"), lax.axis_index("term")
     core = lax.rem(term, 2)
     chip = term // 2
@@ -55,6 +55,12 @@
         dev(sec + 1, jnp.where(cross[1], NZ - 1 - z, z), x, core),
     )
 
+    relay = (sec == LAST, sec == 0)
+    y = lax.rem(sec, CUT)
+    corner = jnp.logical_or(y == 0, y == CUT - 1)
+    across = dev(lax.rem(sec + CUT, 2 * CUT), NZ - 1 - z, x, core)
+    around = dev(sec + CUT - 1 - 2 * y, z, x, core)
+
     loads = [
         pltpu.make_async_copy(psi.at[:, 0], win0.at[pl.ds(2, 2)], load_sem.at[0]),
         pltpu.make_async_copy(psi.at[:, 1], win1.at[pl.ds(2, 2)], load_sem.at[1]),
@@ -72,7 +78,12 @@
         def _():
             pl.semaphore_signal(barrier, inc=1, device_id=ypeer[side], device_id_type=MESH)
 
-    ends = jnp.where(has[0], 1, 0) + jnp.where(has[1], 1, 0)
+    @pl.when(corner)
+    def _():
+        pl.semaphore_signal(barrier, inc=1, device_id=across, device_id_type=MESH)
+        pl.semaphore_signal(barrier, inc=1, device_id=around, device_id_type=MESH)
+
+    ends = jnp.where(has[0], 1, 0) + jnp.where(has[1], 1, 0) + jnp.where(corner, 2, 0)
     pl.semaphore_wait(barrier, 7 + ends)
 
     def remote(src, dst, ssem, rsem, device):
@@ -80,7 +91,9 @@
             src_ref=src, dst_ref=dst, send_sem=ssem, recv_sem=rsem, device_id=device, device_id_type=MESH
         )
 
-    odd = lax.rem(x, 2)
+    odd, zodd = lax.rem(x, 2), lax.rem(z, 2)
+    quarter = [lax.rem(x + 2 * zodd + n, NX) for n in range(NX)]
+    sharers = (xring[0], dev(sec, z + 1 - 2 * zodd, x, core), xring[2])
 
     def block_rows(n):
         return pl.ds(pl.multiple_of(n * QR, QR), QR)
@@ -111,14 +124,30 @@
 
     def e_copy(v, side, h, landing):
         at = side if landing else 1 - side
-        part = piece_rows(x, h)
+        part = piece_rows(quarter[0] if landing else quarter[2], h)
+        if h == 1 and not landing:
+            return remote(psi.at[core, v, part], rbufs[v], esend.at[v, side, h], rrecv.at[v], across)
         return remote(
             psi.at[core, v, part], wins[v].at[spot(at), part], esend.at[v, side, h], erecv.at[v, at, h], ypeer[side]
         )
 
+    def r_copy(v, side):
+        part = piece_rows(quarter[0], 1)
+        return remote(rbufs[v], wins[v].at[spot(side), part], rsend.at[v], erecv.at[v, side, 1], around)
+
+    def r_wait(v):
+        return remote(rbufs[v], rbufs[v], rsend.at[v], rrecv.at[v], across)
+
+    def pass_r(v):
+        for side in (0, 1):
+            @pl.when(relay[side])
+            def _():
+                r_wait(v).wait_recv()
+                r_copy(v, side).start()
+
     def q_copy(v, side, h, k, landing):
-        place = wins[v].at[spot(side), piece_rows(lax.rem(x + 3 - k, NX) if landing else x, h)]
-        return remote(place, place, qsend.at[v, side, 3 * h + k], qrecv.at[v, side, 3 * h + k], xring[k])
+        place = wins[v].at[spot(side), piece_rows(quarter[3 - k if landing else 0], h)]
+        return remote(place, place, qsend.at[v, side, 3 * h + k], qrecv.at[v, side, 3 * h + k], sharers[k])
 
     def pass_on(v, side, part, n):
         place = wins[v].at[spot(side), part]
@@ -129,8 +158,6 @@
         return remote(place, place, fsend.at[v, side, 0], frecv.at[v, side], sibling)
 
     def issue_y(v, j):
-        if j == 2 and not ND:
-            return
         for side in (0, 1):
             @pl.when(direct[side])
             def _():
@@ -143,8 +170,6 @@
                 e_copy(v, side, h, False).start()
 
     def pass_y(v, j):
-        if j == 2 and not ND:
-            return
         for side in (0, 1):
             @pl.when(direct[side])
             def _():
@@ -168,7 +193,7 @@
                 for k in range(3):
                     q_copy(v, side, h, k, False).start()
                 if h == 1:
-                    pass_on(v, side, block_rows(x), 0).start()
+                    pass_on(v, side, block_rows(quarter[0]), 0).start()
 
     def pass_q(v):
         for side in (0, 1):
@@ -177,7 +202,7 @@
                 for k in (0, 2, 1):
                     for h in (0, 1):
                         q_copy(v, side, h, k, True).wait_recv()
-                    pass_on(v, side, block_rows(lax.rem(x + 3 - k, NX)), 1 + k).start()
+                    pass_on(v, side, block_rows(quarter[3 - k]), 1 + k).start()
 
     def finish(v):
         for side in (0, 1):
@@ -190,12 +215,16 @@
             @pl.when(direct[side])
             def _():
                 for j in (0, 1, 2):
-                    if j < 2 or ND:
+                    if True:
                         y_copy(v, side, j, False).wait_send()
                         pass_on(v, side, y_rows(side, j), j).wait_send()
                 for j in (0, 1):
                     h_copy(v, side, j, False).wait_send()
                     pass_on(v, side, shared_rows(0, 0), 3 + j).wait_send()
+
+            @pl.when(relay[side])
+            def _():
+                r_copy(v, side).wait_send()
 
             @pl.when(cross[side])
             def _():
@@ -228,45 +257,41 @@
 
     def products(v):
         for s in range(2):
-            if COMP:
-                compute(v, s)
-            if RS >= 1:
-                exchange(v, s).start()
+            compute(v, s)
+            exchange(v, s).start()
 
     def add_cores(v):
-        for s in range(2 if RS >= 1 else 0):
+        for s in range(2):
             exchange(v, s).wait_recv()
             both = accs[v][s, :, core].astype(f32) + cexs[v][s].astype(f32)
             pairs[v][s] = both.astype(bf16).reshape(NZ, NX, RB, B)
-            if RS >= 2:
-                for k in range(3):
-                    xhop(v, s, k).start()
+            for k in (1, 0, 2):
+                xhop(v, s, k).start()
 
     def add_x(v):
-        for s in range(2 if RS >= 2 else 0):
+        for s in range(2):
             total = pairs[v][s, :, x].astype(f32)
             for k in range(3):
                 xhop(v, s, k).wait_recv()
                 total += xins[v][s, k].astype(f32)
             xsums[v][s] = total.astype(bf16)
-            if RS >= 3:
-                for k in range(3):
-                    zhop(v, s, k).start()
+            for k in range(3):
+                zhop(v, s, k).start()
 
     def add_z(v):
-        for s in range(2 if RS >= 3 else 0):
+        for s in range(2):
             total = xsums[v][s, z].astype(f32)
             for k in range(3):
                 zhop(v, s, k).wait_recv()
                 total += zins[v][s, k].astype(f32)
             out[s, v] = total.astype(bf16)
 
-    if HALO:
-        issue_y(0, 0)
-        issue_e(0, 0)
-        issue_y(0, 1)
-        issue_e(0, 1)
-        issue_y(0, 2)
+    issue_y(0, 0)
+    for v in range(V):
+        for h in (0, 1):
+            issue_e(v, h)
+    issue_y(0, 1)
+    issue_y(0, 2)
     for side in (0, 1):
         @pl.when(jnp.logical_not(has[side]))
         def _():
@@ -278,42 +303,39 @@
         copy.wait()
 
     at_cut = jnp.logical_or(cross[0], cross[1])
-    if HALO:
-        pass_y(0, 0)
-        issue_y(1, 0)
-        pass_e(0, 0)
-        issue_e(1, 0)
-        pass_y(0, 1)
-        issue_y(1, 1)
-        pass_e(0, 1)
-        issue_e(1, 1)
-        pass_x(0, 0)
-        pass_y(0, 2)
-        issue_y(1, 2)
-        pass_e(1, 0)
-        pass_x(0, 1)
-        pass_y(1, 0)
-
-        @pl.when(at_cut)
-        def _():
-            pass_e(1, 1)
-            pass_y(1, 1)
-            pass_q(0)
-
-        finish(0)
+    pass_y(0, 0)
+    issue_y(1, 0)
+    pass_y(0, 1)
+    issue_y(1, 1)
+    pass_r(0)
+    pass_e(0, 0)
+    pass_x(0, 0)
+    pass_x(0, 1)
+    pass_r(1)
+    pass_e(1, 0)
+    pass_e(0, 1)
+    pass_y(0, 2)
+    issue_y(1, 2)
+    pass_y(1, 0)
+
+    @pl.when(at_cut)
+    def _():
+        pass_e(1, 1)
+        pass_y(1, 1)
+        pass_q(0)
+
+    finish(0)
     products(0)
-    if HALO:
-        @pl.when(jnp.logical_not(at_cut))
-        def _():
-            pass_y(1, 1)
+    @pl.when(jnp.logical_not(at_cut))
+    def _():
+        pass_y(1, 1)
 
     add_cores(0)
-    if HALO:
-        pass_x(1, 0)
-        pass_y(1, 2)
-        pass_x(1, 1)
-        pass_q(1)
-        finish(1)
+    pass_x(1, 0)
+    pass_y(1, 2)
+    pass_x(1, 1)
+    pass_q(1)
+    finish(1)
     products(1)
     add_cores(1)
     add_x(0)
@@ -322,17 +344,13 @@
     add_z(1)
 
     for v in range(V):
-        if HALO:
-            drain(v)
+        drain(v)
         for s in range(2):
-            if RS >= 1:
-                exchange(v, s).wait_send()
-            if RS >= 2:
-                for k in range(3):
-                    xhop(v, s, k).wait_send()
-            if RS >= 3:
-                for k in range(3):
-                    zhop(v, s, k).wait_send()
+            exchange(v, s).wait_send()
+            for k in range(3):
+                xhop(v, s, k).wait_send()
+            for k in range(3):
+                zhop(v, s, k).wait_send()
 
 
 def local(psi, left_ops, right_ops, shift, live):
@@ -346,6 +364,7 @@
         in_specs=[smem, smem, hbm, hbm, hbm],
         out_specs=pl.BlockSpec(memory_space=pltpu.VMEM),
         scratch_shapes=[pltpu.VMEM((2, B, B), bf16)] * 2
+        + per_vector((QH, B))
         + per_vector((6, B, B))
         + per_vector((2, NX * NZ, 2, RB, B))
         + per_vector((2, NX * NZ, RB, B))
@@ -357,6 +376,7 @@
         + [dma((V, 2, 3))] * 2
         + [dma((V, 2, 2))] * 2
         + [dma((V, 2, 2))] * 2
+        + [dma((V,))] * 2
         + [dma((V, 2, 6))] * 2
         + [dma((V, 2, 5)), dma((V, 2))]
         + [dma((V, 2))] * 2

time: 50.4 us -> 49.4 us (0.980)
  Pallas kernels: 48.3 us -> 47.2 us
    pallas_call x1, Pallas kernels: 48.3 us -> 47.2 us  [local(): pl.pallas_call(kernel, out_shape=jax.ShapeDtypeStruct((2, V, RB, B), bf16...]
where the time goes in v4:
time: 49.4 us; the launch traced here: 49.2 us
  Pallas kernels  47.2 us (96%)
  between operations  1.3 us (3%)
  local copies, waits for them, and re-layouts  0.63 us (1%)
    pallas_call x1, Pallas kernels, local(): pl.pallas_call(kernel, out_shape=jax.ShapeDtypeStruct((2, V, RB, B), bf16...  47.2 us

profile of v4, /device:TPU:56, one launch (start us, length us, event | category | flops | bytes accessed | tf_op | source)
XLA Modules:
  0.0 49.2 jit_solution(14491886985136013271)
XLA Ops:
  1.3 47.2 %sigma.1 = bf16[2,2,16,512]{3,2,1,0:T(8,128)(2,1)S(1)} custom-call(s32[1]{0:T(128)S(6)} %copy.7.shift_ref, s32[1]{0:T(128)S(6)} %copy.8.live_ref, bf16[2,2,512,512]{3,2,1,0:T(8,128)(2,1)} %psi.1, bf16[1,2,512,512]{3,2,1,0:T(8,128)(2,1)} %left.1, bf16[1,2,512,512]{3,2,1,0:T(8,128)(2,1)} %right.1), custom_call_target="tpu_custom_call" | custom-call | tf_op jit(solution)/shard_map/sigma/pallas_call | solution.py:361
  48.5 0.6 %copy.9 = bf16[2,2,16,512]{3,2,1,0:T(8,128)(2,1)} copy(bf16[2,2,16,512]{3,2,1,0:T(8,128)(2,1)S(1)} %sigma.1) | data formatting | bytes 131072

commit v5 on v4

--- a/solution.py
+++ b/solution.py
@@ -332,9 +332,9 @@
 
     add_cores(0)
     pass_x(1, 0)
-    pass_y(1, 2)
     pass_x(1, 1)
     pass_q(1)
+    pass_y(1, 2)
     finish(1)
     products(1)
     add_cores(1)

time: 49.4 us -> 49.4 us (level)
  no operation moved by 1% of the time
where the time goes in v5:
time: 49.4 us; the launch traced here: 49.2 us
  Pallas kernels  47.2 us (96%)
  between operations  1.3 us (3%)
  local copies, waits for them, and re-layouts  0.63 us (1%)
    pallas_call x1, Pallas kernels, local(): pl.pallas_call(kernel, out_shape=jax.ShapeDtypeStruct((2, V, RB, B), bf16...  47.2 us

profile of v5, /device:TPU:56, one launch (start us, length us, event | category | flops | bytes accessed | tf_op | source)
XLA Modules:
  0.0 49.2 jit_solution(15925969456538328498)
XLA Ops:
  1.3 47.2 %sigma.1 = bf16[2,2,16,512]{3,2,1,0:T(8,128)(2,1)S(1)} custom-call(s32[1]{0:T(128)S(6)} %copy.7.shift_ref, s32[1]{0:T(128)S(6)} %copy.8.live_ref, bf16[2,2,512,512]{3,2,1,0:T(8,128)(2,1)} %psi.1, bf16[1,2,512,512]{3,2,1,0:T(8,128)(2,1)} %left.1, bf16[1,2,512,512]{3,2,1,0:T(8,128)(2,1)} %right.1), custom_call_target="tpu_custom_call" | custom-call | tf_op jit(solution)/shard_map/sigma/pallas_call | solution.py:361
  48.5 0.6 %copy.9 = bf16[2,2,16,512]{3,2,1,0:T(8,128)(2,1)} copy(bf16[2,2,16,512]{3,2,1,0:T(8,128)(2,1)S(1)} %sigma.1) | data formatting | bytes 131072
